TPU v7x, 256 devices: a whole 4x4x8 slice. The times are simulated.
256 devices in a mesh: mem: 16 (over z, x_lo), lon: 16 (over x_hi, y, core).
Axes of the slice: x: 4 (x_hi: 2, x_lo: 2; x = x_hi * 2 + x_lo), y: 4, z: 8, core: 2. Of those that a mesh axis runs over, the one named last changes fastest.
Arguments:
- state: bfloat16 [256, 65536], P('mem', 'lon'), may hold values from -6 to 6
- hx: bfloat16 [512, 256, 128], P('lon'), may hold values from -6 to 6
- obs_value: float32 [512, 128], P('lon'), may hold values from -10 to 10
- obs_rinv: float32 [512, 128], P('lon'), may hold values from 0.3 to 3
- obs_count: int32 [512], P('lon'), may hold values from 1 to 128
- loc_pattern: int32 [512, 8], P('lon'), may hold values from 0 to 95, as said below
Outputs:
- analysis: bfloat16 [256, 65536], P('mem', 'lon')
Inputs may be any that keep to these rules, and one draw needn't show every extreme that they name: obs_count[n] is how many of block n's first observations are valid; the rest are ignored. Each row of loc_pattern holds 8 different window positions out of 96: the previous region's blocks, the patch's own region's blocks, the next region's blocks, around the closed longitude loop.
All inputs are finite; a program needn't handle non-finite values.
Results may differ from a plain program's by a relative error of at most 0.0065.
Values may be sent and summed in bfloat16 or wider, within the bound.
A program may use at most 64 MiB of HBM per device.

v0:
```python
import jax
import jax.numpy as jnp
from jax import lax
from jax.sharding import PartitionSpec as P

PAT_DEV = 2
USE = 8
ITERS = 6


def extended(value, sides, width):
    for axis, dim in sides:
        count, length = (lax.axis_size(axis), value.shape[dim])
        up = [(i, (i + 1) % count) for i in range(count)]
        down = [(j, i) for i, j in up]
        last = lax.slice_in_dim(value, length - width, length, axis=dim)
        first = lax.slice_in_dim(value, 0, width, axis=dim)
        before = lax.ppermute(last, axis, up)
        after = lax.ppermute(first, axis, down)
        value = jnp.concatenate([before, value, after], axis=dim)
    return value


def body(state, hx, obs_value, obs_rinv, obs_count, loc_pattern):
    high = lax.Precision.HIGHEST
    blocks = hx.shape[0]
    members = hx.shape[1]
    width_obs = hx.shape[2]
    mem_total = lax.axis_size("mem")
    mem_here = lax.axis_index("mem")
    region_patches = mem_total * PAT_DEV
    obs_mean = jnp.sum(hx, axis=1, dtype=jnp.float32) / members
    obs_pert = (hx.astype(jnp.float32) - obs_mean[:, None, :]).astype(jnp.bfloat16)
    valid = lax.broadcasted_iota(jnp.int32, (blocks, width_obs), 1) < obs_count[:, None]
    weight = jnp.where(valid, obs_rinv, jnp.float32(0.0))
    stats = jnp.stack([weight, weight * (obs_value - obs_mean)], axis=1).astype(jnp.bfloat16)
    picks = lax.dynamic_slice_in_dim(loc_pattern, mem_here * PAT_DEV, PAT_DEV, 0)
    ranks = (mem_here * PAT_DEV + jnp.arange(PAT_DEV, dtype=jnp.int32)).astype(jnp.float32)
    offset = (
        (picks.astype(jnp.float32) + 0.5) / blocks - 1.0 - (ranks[:, None] + 0.5) / region_patches
    )
    taper = jnp.exp(-0.5 * offset * offset)
    eye = jnp.eye(members, dtype=jnp.float32)
    system = jnp.broadcast_to((members - 1.0) * eye, (PAT_DEV, members, members))
    forcing = jnp.zeros((PAT_DEV, members), jnp.float32)
    window_pert, window_stats = (
        extended(obs_pert, (("lon", 0),), blocks),
        extended(stats, (("lon", 0),), blocks),
    )
    for slot in range(USE):
        chosen = picks[:, slot]
        picked_pert = window_pert[chosen]
        picked_stats = window_stats[chosen]
        scaled = (
            picked_stats[:, 0, None, :].astype(jnp.float32) * picked_pert.astype(jnp.float32)
        ).astype(jnp.bfloat16)
        gram = jnp.einsum("pkb,plb->pkl", picked_pert, scaled, preferred_element_type=jnp.float32)
        vec = jnp.einsum(
            "pkb,pb->pk", picked_pert, picked_stats[:, 1], preferred_element_type=jnp.float32
        )
        system = system + taper[:, slot, None, None] * gram
        forcing = forcing + taper[:, slot, None] * vec
    scale = jnp.sqrt(jnp.sum(system * system, axis=(1, 2)))
    iterate = system / scale[:, None, None]
    root = jnp.broadcast_to(eye, (PAT_DEV, members, members))
    for step in range(ITERS):
        factor = 1.5 * eye - 0.5 * jnp.einsum("pij,pjk->pik", root, iterate, precision=high)
        iterate = jnp.einsum("pij,pjk->pik", iterate, factor, precision=high)
        root = jnp.einsum("pij,pjk->pik", factor, root, precision=high)
    root = root / jnp.sqrt(scale)[:, None, None]
    inner = jnp.einsum("pij,pj->pi", root, forcing, precision=high)
    mean_weight = jnp.einsum("pij,pj->pi", root, inner, precision=high)
    transform = jnp.sqrt(jnp.float32(members - 1.0)) * root + mean_weight[:, :, None]
    local_members = state.shape[0]
    grid = state.reshape(local_members, region_patches, -1)
    gathered = lax.all_to_all(grid, "mem", split_axis=1, concat_axis=0, tiled=True)
    state_mean = jnp.sum(gathered, axis=0, dtype=jnp.float32) / members
    deviation = gathered.astype(jnp.float32) - state_mean[None]
    updated = state_mean[None] + jnp.einsum("pkl,kpt->lpt", transform, deviation, precision=high)
    result = lax.all_to_all(
        updated.astype(jnp.bfloat16), "mem", split_axis=0, concat_axis=1, tiled=True
    )
    return result.reshape(local_members, -1)


def solution(mesh):
    in_specs = (
        P("mem", "lon"),
        P("lon", None, None),
        P("lon", None),
        P("lon", None),
        P("lon"),
        P("lon", None),
    )
    out_specs = P("mem", "lon")
    return jax.shard_map(body, mesh=mesh, in_specs=in_specs, out_specs=out_specs, check_vma=False)
```

profile of v0, /device:TPU:4, one launch (start us, length us, event | category | flops | bytes accessed | tf_op | source)
XLA Modules:
  0.0 112.8 jit_solution(15731651959545263145)
XLA Ops:
  0.0 2.0 %convert_reduce_fusion = f32[32,128]{1,0:T(8,128)S(1)} fusion(bf16[32,256,128]{2,1,0:T(8,128)(2,1)} %param.7), kind=kLoop, calls=%fused_computation.18 | loop fusion | flops 2093056 | bytes 2113536 | tf_op jit(solution)/shard_map/reduce_sum | solution.py:32
  2.0 0.8 fusion.38
  2.8 0.8 fusion.39
  3.8 5.3 %collective-permute-start.3 = (bf16[32,2,128]{2,1,0:T(2,128)(2,1)S(1)}, bf16[32,2,128]{2,1,0:T(2,128)(2,1)S(1)}, u32[]{:S(2)}, u32[]{:S(2)}) collective-permute-start(bf16[32,2,128]{2,1,0:T(2,128)(2,1)S(1)} %pad_maximum_fusion.2), channel_id=1, source_target_pairs={{1,0},{2,1},{3,2},{4,3},{5,4},{6,5},{7,6},{8,7},{9,8},{10,9},{11,1... | collective-permute-start | bytes 49160 | tf_op jit(solution)/shard_map/ppermute | solution.py:19
  9.1 2.2 %fusion = bf16[32,256,128]{2,1,0:T(8,128)(2,1)S(1)} fusion(bf16[32,256,128]{2,1,0:T(8,128)(2,1)} %param.7, f32[32,128]{1,0:T(8,128)S(1)} %get-tuple-element.8), kind=kLoop, calls=%fused_computation.19 | loop fusion | flops 3145728 | bytes 4210688 | tf_op jit(solution)/shard_map/convert_element_type | solution.py:33
  11.4 5.3 %collective-permute-start.1 = (bf16[32,256,128]{2,1,0:T(8,128)(2,1)S(1)}, bf16[32,256,128]{2,1,0:T(8,128)(2,1)}, u32[]{:S(2)}, u32[]{:S(2)}) collective-permute-start(bf16[32,256,128]{2,1,0:T(8,128)(2,1)S(1)} %fusion), channel_id=1, source_target_pairs={{1,0},{2,1},{3,2},{4,3},{5,4},{6,5},{7,6},{8,7},{9,8},{10,9},{11,1... | collective-permute-start | bytes 6291464 | tf_op jit(solution)/shard_map/ppermute | solution.py:19
  16.7 0.7 copy_bitcast_fusion
  17.4 9.2 %all-to-all-start = ((bf16[16,32,128]{2,0,1:T(8,128)(2,1)}), bf16[16,32,128]{2,0,1:T(8,128)(2,1)S(1)}, u32[]{:S(2)}, u32[]{:S(2)}) async-start(bf16[16,32,128]{2,0,1:T(8,128)(2,1)} %copy_bitcast_fusion), calls=%async_computation | async-start | bytes 262144 | tf_op jit(solution)/shard_map/all_to_all | solution.py:76
  27.0 0.6 gather_fusion.13
  27.6 0.6 gather_fusion.11
  28.2 0.6 gather_fusion.9
  28.7 0.6 gather_fusion.7
  29.3 0.6 gather_fusion.5
  29.9 0.6 gather_fusion.3
  30.4 0.6 gather_fusion.15
  31.1 0.6 gather_fusion.1
  31.7 11.7 %all-to-all-done = bf16[16,32,128]{2,0,1:T(8,128)(2,1)S(1)} async-done(((bf16[16,32,128]{2,0,1:T(8,128)(2,1)}), bf16[16,32,128]{2,0,1:T(8,128)(2,1)S(1)}, u32[]{:S(2)}, u32[]{:S(2)}) %all-to-all-start) | async-done | bytes 131104 | tf_op jit(solution)/shard_map/all_to_all | solution.py:76
  43.5 0.7 bitcast_subtract_fusion
  44.2 5.5 %pad_maximum_fusion = bf16[96,256,128]{2,1,0:T(8,128)(2,1)} fusion(bf16[32,256,128]{2,1,0:T(8,128)(2,1)} %collective-permute-done.1, bf16[32,256,128]{2,1,0:T(8,128)(2,1)S(1)} %fusion, bf16[32,256,128]{2,1,0:T(8,128)(2,1)} %collective-permute-done), kind=kLoop, calls=%fused_computation.16 | loop fusion | flops 6291456 | bytes 12582912 | tf_op jit(solution)/shard_map/concatenate | solution.py:20
  49.8 3.4 %gather_fusion.12 = bf16[2,256,128]{2,1,0:T(8,128)(2,1)S(1)} fusion(bf16[96,256,128]{2,1,0:T(8,128)(2,1)} %pad_maximum_fusion, s32[1024]{0:T(1024)S(1)} %get-tuple-element.30), kind=kCustom, calls=%fused_computation.12 | custom fusion | bytes 262152 | tf_op jit(solution)/shard_map/gather | solution.py:52
  53.1 3.4 %gather_fusion.10 = bf16[2,256,128]{2,1,0:T(8,128)(2,1)S(1)} fusion(bf16[96,256,128]{2,1,0:T(8,128)(2,1)} %pad_maximum_fusion, s32[1024]{0:T(1024)S(1)} %get-tuple-element.31), kind=kCustom, calls=%fused_computation.10 | custom fusion | bytes 262152 | tf_op jit(solution)/shard_map/gather | solution.py:52
  56.5 3.4 %gather_fusion.8 = bf16[2,256,128]{2,1,0:T(8,128)(2,1)S(1)} fusion(bf16[96,256,128]{2,1,0:T(8,128)(2,1)} %pad_maximum_fusion, s32[1024]{0:T(1024)S(1)} %get-tuple-element.32), kind=kCustom, calls=%fused_computation.8 | custom fusion | bytes 262152 | tf_op jit(solution)/shard_map/gather | solution.py:52
  59.8 3.4 %gather_fusion.6 = bf16[2,256,128]{2,1,0:T(8,128)(2,1)S(1)} fusion(bf16[96,256,128]{2,1,0:T(8,128)(2,1)} %pad_maximum_fusion, s32[1024]{0:T(1024)S(1)} %get-tuple-element.33), kind=kCustom, calls=%fused_computation.6 | custom fusion | bytes 262152 | tf_op jit(solution)/shard_map/gather | solution.py:52
  63.2 3.4 %gather_fusion.4 = bf16[2,256,128]{2,1,0:T(8,128)(2,1)S(1)} fusion(bf16[96,256,128]{2,1,0:T(8,128)(2,1)} %pad_maximum_fusion, s32[1024]{0:T(1024)S(1)} %get-tuple-element.34), kind=kCustom, calls=%fused_computation.4 | custom fusion | bytes 262152 | tf_op jit(solution)/shard_map/gather | solution.py:52
  66.6 3.4 %gather_fusion.2 = bf16[2,256,128]{2,1,0:T(8,128)(2,1)S(1)} fusion(bf16[96,256,128]{2,1,0:T(8,128)(2,1)} %pad_maximum_fusion, s32[1024]{0:T(1024)S(1)} %get-tuple-element.35), kind=kCustom, calls=%fused_computation.2 | custom fusion | bytes 262152 | tf_op jit(solution)/shard_map/gather | solution.py:52
  69.9 3.4 %gather_fusion = bf16[2,256,128]{2,1,0:T(8,128)(2,1)S(1)} fusion(bf16[96,256,128]{2,1,0:T(8,128)(2,1)} %pad_maximum_fusion, s32[1024]{0:T(1024)S(1)} %get-tuple-element.36), kind=kCustom, calls=%fused_computation | custom fusion | bytes 262152 | tf_op jit(solution)/shard_map/gather | solution.py:52
  73.3 3.4 %gather_fusion.14 = bf16[2,256,128]{2,1,0:T(8,128)(2,1)S(1)} fusion(bf16[96,256,128]{2,1,0:T(8,128)(2,1)} %pad_maximum_fusion, s32[1024]{0:T(1024)S(1)} %get-tuple-element.29), kind=kCustom, calls=%fused_computation.14 | custom fusion | bytes 262152 | tf_op jit(solution)/shard_map/gather | solution.py:52
  76.8 0.1 fusion.55
  76.9 0.1 fusion.56
  77.1 0.1 fusion.57
  77.2 0.1 fusion.58
  77.4 0.1 fusion.59
  77.5 0.1 fusion.60
  77.7 0.1 fusion.53
  77.8 0.2 convolution_multiply_fusion.10
  78.1 0.2 convolution_multiply_fusion.11
  78.3 0.2 convolution_multiply_fusion.12
  78.6 0.2 convolution_multiply_fusion.7
  78.8 0.2 convolution_multiply_fusion.8
  79.0 0.2 convolution_multiply_fusion.9
  79.3 0.2 convolution_multiply_fusion.6
  79.5 0.5 multiply_reduce_fusion
  80.0 0.7 fusion.6
  80.7 0.7 fusion.35
  81.4 0.6 fusion.21
  82.1 0.7 fusion.5
  82.7 0.7 fusion.71
  83.4 0.7 fusion.70
  84.0 0.7 fusion.4
  84.7 0.7 fusion.73
  85.4 0.7 fusion.72
  86.0 0.7 fusion.3
  86.7 0.7 fusion.75
  87.4 0.7 fusion.74
  88.0 0.7 fusion.2
  88.7 0.7 fusion.77
  89.3 0.7 fusion.76
  90.0 0.9 fusion.1
  90.9 0.7 convolution_divide_fusion
  91.6 0.5 fusion.51
  92.2 0.6 fusion.49
  92.8 0.7 fusion.16
  93.6 18.3 %all_to_all.24 = bf16[256,2,128]{2,1,0:T(2,128)(2,1)S(1)} all-to-all(bf16[256,2,128]{2,1,0:T(2,128)(2,1)S(1)} %copy.46), channel_id=1, replica_groups=mesh['mem'=16,'lon'=16] {'mem'}, dimensions={0} | all-to-all | bytes 262144 | tf_op jit(solution)/shard_map/all_to_all | solution.py:80
  112.0 0.7 reshape.53
  (48 shorter events, 1.2 us)
Async XLA Ops:
  0.0 16.7 %copy-start = (bf16[16,4096]{1,0:T(8,128)(2,1)S(1)}, bf16[16,4096]{1,0:T(8,128)(2,1)}, u32[]{:S(2)}) copy-start(bf16[16,4096]{1,0:T(8,128)(2,1)} %param.6) | copy-start | bytes 393220
  0.0 26.7 %copy-start.2 = (s32[32,8]{0,1:T(8,128)S(1)}, s32[32,8]{0,1:T(8,128)}, u32[]{:S(2)}) copy-start(s32[32,8]{0,1:T(8,128)} %param.11) | copy-start | bytes 3076
  3.7 23.2 %collective-permute-start.2 = (bf16[32,2,128]{2,1,0:T(2,128)(2,1)S(1)}, bf16[32,2,128]{2,1,0:T(2,128)(2,1)S(1)}, u32[]{:S(2)}, u32[]{:S(2)}) collective-permute-start(bf16[32,2,128]{2,1,0:T(2,128)(2,1)S(1)} %pad_maximum_fusion.2), channel_id=1, source_target_pairs={{0,1},{1,2},{2,3},{3,4},{4,5},{5,6},{6,7},{7,8},{8,9},{9,10},{10,1... | collective-permute-start | bytes 49160 | tf_op jit(solution)/shard_map/ppermute | solution.py:18
  3.8 23.2 %collective-permute-start.3 = (bf16[32,2,128]{2,1,0:T(2,128)(2,1)S(1)}, bf16[32,2,128]{2,1,0:T(2,128)(2,1)S(1)}, u32[]{:S(2)}, u32[]{:S(2)}) collective-permute-start(bf16[32,2,128]{2,1,0:T(2,128)(2,1)S(1)} %pad_maximum_fusion.2), channel_id=1, source_target_pairs={{1,0},{2,1},{3,2},{4,3},{5,4},{6,5},{7,6},{8,7},{9,8},{10,9},{11,1... | collective-permute-start | bytes 49160 | tf_op jit(solution)/shard_map/ppermute | solution.py:19
  11.3 32.9 %collective-permute-start = (bf16[32,256,128]{2,1,0:T(8,128)(2,1)S(1)}, bf16[32,256,128]{2,1,0:T(8,128)(2,1)}, u32[]{:S(2)}, u32[]{:S(2)}) collective-permute-start(bf16[32,256,128]{2,1,0:T(8,128)(2,1)S(1)} %fusion), channel_id=1, source_target_pairs={{0,1},{1,2},{2,3},{3,4},{4,5},{5,6},{6,7},{7,8},{8,9},{9,10},{10,1... | collective-permute-start | bytes 6291464 | tf_op jit(solution)/shard_map/ppermute | solution.py:18
  11.4 32.8 %collective-permute-start.1 = (bf16[32,256,128]{2,1,0:T(8,128)(2,1)S(1)}, bf16[32,256,128]{2,1,0:T(8,128)(2,1)}, u32[]{:S(2)}, u32[]{:S(2)}) collective-permute-start(bf16[32,256,128]{2,1,0:T(8,128)(2,1)S(1)} %fusion), channel_id=1, source_target_pairs={{1,0},{2,1},{3,2},{4,3},{5,4},{6,5},{7,6},{8,7},{9,8},{10,9},{11,1... | collective-permute-start | bytes 6291464 | tf_op jit(solution)/shard_map/ppermute | solution.py:19
  17.4 25.9 %all-to-all-start = ((bf16[16,32,128]{2,0,1:T(8,128)(2,1)}), bf16[16,32,128]{2,0,1:T(8,128)(2,1)S(1)}, u32[]{:S(2)}, u32[]{:S(2)}) async-start(bf16[16,32,128]{2,0,1:T(8,128)(2,1)} %copy_bitcast_fusion), calls=%async_computation | async-start | bytes 262144 | tf_op jit(solution)/shard_map/all_to_all | solution.py:76
  86.7 6.1 %copy-start.1 = (f32[256,2,128]{2,0,1:T(8,128)S(1)}, f32[256,2,128]{2,0,1:T(8,128)}, u32[]{:S(2)}) copy-start(f32[256,2,128]{2,0,1:T(8,128)} %bitcast_subtract_fusion) | copy-start | bytes 786436
where the time goes:
time: 114 us; the launch traced here: 113 us
  local copies, waits for them, and re-layouts  33.2 us (29%)
  starting transfers between devices  20.1 us (18%)
  blocking collectives  18.3 us (16%)
  matrix products  16.5 us (14%)
  other arithmetic  12.5 us (11%)
  waiting for transfers between devices  11.7 us (10%)
    gather x8, local copies, waits for them, and re-layouts, body(): picked_pert = window_pert[chosen]  26.9 us
    all_to_all x1, blocking collectives, body(): lax.all_to_all(updated.astype(jnp.bfloat16), 'mem', split_axis=0, concat_...  18.3 us
    all_to_all x1, waiting for transfers between devices, body(): lax.all_to_all(grid, 'mem', split_axis=1, concat_axis=0, tiled=True)  11.7 us
    ppermute x2, starting transfers between devices, extended(): after = lax.ppermute(first, axis, down)  10.7 us
    all_to_all x1, starting transfers between devices, body(): lax.all_to_all(grid, 'mem', split_axis=1, concat_axis=0, tiled=True)  9.2 us
    concatenate x2, other arithmetic, extended(): value = jnp.concatenate([before, value, after], axis=dim)  5.6 us
    gather x8, local copies, waits for them, and re-layouts, body(): picked_stats = window_stats[chosen]  4.57 us
    dot_general x6, matrix products, body(): jnp.einsum('pij,pjk->pik', root, iterate, precision=high)  4.22 us
  transfers between devices with their start and end apart: 5, of which 1 were waited for; matrix products, arithmetic and copies ran while one was open for 8% of the time, Pallas kernels for 0%

commit v1 on v0

--- a/solution.py
+++ b/solution.py
@@ -77,8 +77,14 @@
     state_mean = jnp.sum(gathered, axis=0, dtype=jnp.float32) / members
     deviation = gathered.astype(jnp.float32) - state_mean[None]
     updated = state_mean[None] + jnp.einsum("pkl,kpt->lpt", transform, deviation, precision=high)
-    result = lax.all_to_all(
-        updated.astype(jnp.bfloat16), "mem", split_axis=0, concat_axis=1, tiled=True
+    result = jnp.concatenate(
+        lax.all_to_all(
+            jnp.stack(jnp.split(updated.astype(jnp.bfloat16), lax.axis_size("mem"), axis=0)),
+            "mem",
+            0,
+            0,
+        ),
+        axis=1,
     )
     return result.reshape(local_members, -1)
 

time: 114 us -> 115 us (level)
  local copies, waits for them, and re-layouts: 33.2 us -> 34.9 us
    another operation x0 -> x19, local copies, waits for them, and re-layouts: none -> 2.48 us  [the longest x18 1.75 us: body(): jnp.stack(jnp.split(updated.astype(jnp.bfloat16), lax.axis_size('mem'), a...]
  transfers between devices with their start and end apart: 5 -> 5, of which waited for: 1 -> 1; matrix products, arithmetic and copies ran while one was open for 8% -> 7% of each run, Pallas kernels for 0% -> 0%
where the time goes in v1:
time: 115 us
  local copies, waits for them, and re-layouts  34.9 us (30%)
  starting transfers between devices  20.1 us (17%)
  blocking collectives  18.3 us (16%)
  matrix products  16.5 us (14%)
  other arithmetic  12.6 us (11%)
  waiting for transfers between devices  11.7 us (10%)
    gather x8, local copies, waits for them, and re-layouts, body(): picked_pert = window_pert[chosen]  26.9 us
    all_to_all x1, blocking collectives, body(): lax.all_to_all(jnp.stack(jnp.split(updated.astype(jnp.bfloat16), lax.axis...  18.3 us
    all_to_all x1, waiting for transfers between devices, body(): lax.all_to_all(grid, 'mem', split_axis=1, concat_axis=0, tiled=True)  11.7 us
    ppermute x2, starting transfers between devices, extended(): after = lax.ppermute(first, axis, down)  10.7 us
    all_to_all x1, starting transfers between devices, body(): lax.all_to_all(grid, 'mem', split_axis=1, concat_axis=0, tiled=True)  9.2 us
    concatenate x2, other arithmetic, extended(): value = jnp.concatenate([before, value, after], axis=dim)  5.66 us
    gather x8, local copies, waits for them, and re-layouts, body(): picked_stats = window_stats[chosen]  4.57 us
    dot_general x6, matrix products, body(): jnp.einsum('pij,pjk->pik', root, iterate, precision=high)  4.22 us
  transfers between devices with their start and end apart: 5, of which 1 were waited for; matrix products, arithmetic and copies ran while one was open for 7% of the time, Pallas kernels for 0%

profile of v1, /device:TPU:4, one launch (start us, length us, event | category | flops | bytes accessed | tf_op | source)
XLA Modules:
  0.0 114.6 jit_solution(14868526098098698818)
XLA Ops:
  0.0 2.0 %convert_reduce_fusion = f32[32,128]{1,0:T(8,128)S(1)} fusion(bf16[32,256,128]{2,1,0:T(8,128)(2,1)} %param.7), kind=kLoop, calls=%fused_computation.18 | loop fusion | flops 2093056 | bytes 2113536 | tf_op jit(solution)/shard_map/reduce_sum | solution.py:32
  2.0 0.8 fusion.38
  2.8 0.8 fusion.39
  3.8 5.3 %collective-permute-start.3 = (bf16[32,2,128]{2,1,0:T(2,128)(2,1)S(1)}, bf16[32,2,128]{2,1,0:T(2,128)(2,1)S(1)}, u32[]{:S(2)}, u32[]{:S(2)}) collective-permute-start(bf16[32,2,128]{2,1,0:T(2,128)(2,1)S(1)} %pad_maximum_fusion.2), channel_id=1, source_target_pairs={{1,0},{2,1},{3,2},{4,3},{5,4},{6,5},{7,6},{8,7},{9,8},{10,9},{11,1... | collective-permute-start | bytes 49160 | tf_op jit(solution)/shard_map/ppermute | solution.py:19
  9.1 2.2 %fusion = bf16[32,256,128]{2,1,0:T(8,128)(2,1)S(1)} fusion(bf16[32,256,128]{2,1,0:T(8,128)(2,1)} %param.7, f32[32,128]{1,0:T(8,128)S(1)} %get-tuple-element.24), kind=kLoop, calls=%fused_computation.19 | loop fusion | flops 3145728 | bytes 4210688 | tf_op jit(solution)/shard_map/convert_element_type | solution.py:33
  11.4 5.3 %collective-permute-start.1 = (bf16[32,256,128]{2,1,0:T(8,128)(2,1)S(1)}, bf16[32,256,128]{2,1,0:T(8,128)(2,1)}, u32[]{:S(2)}, u32[]{:S(2)}) collective-permute-start(bf16[32,256,128]{2,1,0:T(8,128)(2,1)S(1)} %fusion), channel_id=1, source_target_pairs={{1,0},{2,1},{3,2},{4,3},{5,4},{6,5},{7,6},{8,7},{9,8},{10,9},{11,1... | collective-permute-start | bytes 6291464 | tf_op jit(solution)/shard_map/ppermute | solution.py:19
  16.7 0.7 copy_bitcast_fusion
  17.4 9.2 %all-to-all-start = ((bf16[16,32,128]{2,0,1:T(8,128)(2,1)}), bf16[16,32,128]{2,0,1:T(8,128)(2,1)S(1)}, u32[]{:S(2)}, u32[]{:S(2)}) async-start(bf16[16,32,128]{2,0,1:T(8,128)(2,1)} %copy_bitcast_fusion), calls=%async_computation | async-start | bytes 262144 | tf_op jit(solution)/shard_map/all_to_all | solution.py:76
  27.0 0.6 gather_fusion.13
  27.6 0.6 gather_fusion.11
  28.2 0.6 gather_fusion.9
  28.7 0.6 gather_fusion.7
  29.3 0.6 gather_fusion.5
  29.9 0.6 gather_fusion.3
  30.4 0.6 gather_fusion.15
  31.1 0.6 gather_fusion.1
  31.7 11.7 %all-to-all-done = bf16[16,32,128]{2,0,1:T(8,128)(2,1)S(1)} async-done(((bf16[16,32,128]{2,0,1:T(8,128)(2,1)}), bf16[16,32,128]{2,0,1:T(8,128)(2,1)S(1)}, u32[]{:S(2)}, u32[]{:S(2)}) %all-to-all-start) | async-done | bytes 131104 | tf_op jit(solution)/shard_map/all_to_all | solution.py:76
  43.5 0.7 bitcast_subtract_fusion
  44.2 5.6 %pad_maximum_fusion = bf16[96,256,128]{2,1,0:T(8,128)(2,1)} fusion(bf16[32,256,128]{2,1,0:T(8,128)(2,1)} %collective-permute-done.1, bf16[32,256,128]{2,1,0:T(8,128)(2,1)S(1)} %fusion, bf16[32,256,128]{2,1,0:T(8,128)(2,1)} %collective-permute-done), kind=kLoop, calls=%fused_computation.16 | loop fusion | flops 6291456 | bytes 12582912 | tf_op jit(solution)/shard_map/concatenate | solution.py:20
  49.8 3.4 %gather_fusion.12 = bf16[2,256,128]{2,1,0:T(8,128)(2,1)S(1)} fusion(bf16[96,256,128]{2,1,0:T(8,128)(2,1)} %pad_maximum_fusion, s32[1024]{0:T(1024)S(1)} %get-tuple-element.46), kind=kCustom, calls=%fused_computation.12 | custom fusion | bytes 262152 | tf_op jit(solution)/shard_map/gather | solution.py:52
  53.2 3.4 %gather_fusion.10 = bf16[2,256,128]{2,1,0:T(8,128)(2,1)S(1)} fusion(bf16[96,256,128]{2,1,0:T(8,128)(2,1)} %pad_maximum_fusion, s32[1024]{0:T(1024)S(1)} %get-tuple-element.47), kind=kCustom, calls=%fused_computation.10 | custom fusion | bytes 262152 | tf_op jit(solution)/shard_map/gather | solution.py:52
  56.5 3.4 %gather_fusion.8 = bf16[2,256,128]{2,1,0:T(8,128)(2,1)S(1)} fusion(bf16[96,256,128]{2,1,0:T(8,128)(2,1)} %pad_maximum_fusion, s32[1024]{0:T(1024)S(1)} %get-tuple-element.48), kind=kCustom, calls=%fused_computation.8 | custom fusion | bytes 262152 | tf_op jit(solution)/shard_map/gather | solution.py:52
  59.9 3.4 %gather_fusion.6 = bf16[2,256,128]{2,1,0:T(8,128)(2,1)S(1)} fusion(bf16[96,256,128]{2,1,0:T(8,128)(2,1)} %pad_maximum_fusion, s32[1024]{0:T(1024)S(1)} %get-tuple-element.49), kind=kCustom, calls=%fused_computation.6 | custom fusion | bytes 262152 | tf_op jit(solution)/shard_map/gather | solution.py:52
  63.3 3.4 %gather_fusion.4 = bf16[2,256,128]{2,1,0:T(8,128)(2,1)S(1)} fusion(bf16[96,256,128]{2,1,0:T(8,128)(2,1)} %pad_maximum_fusion, s32[1024]{0:T(1024)S(1)} %get-tuple-element.50), kind=kCustom, calls=%fused_computation.4 | custom fusion | bytes 262152 | tf_op jit(solution)/shard_map/gather | solution.py:52
  66.6 3.4 %gather_fusion.2 = bf16[2,256,128]{2,1,0:T(8,128)(2,1)S(1)} fusion(bf16[96,256,128]{2,1,0:T(8,128)(2,1)} %pad_maximum_fusion, s32[1024]{0:T(1024)S(1)} %get-tuple-element.51), kind=kCustom, calls=%fused_computation.2 | custom fusion | bytes 262152 | tf_op jit(solution)/shard_map/gather | solution.py:52
  70.0 3.4 %gather_fusion = bf16[2,256,128]{2,1,0:T(8,128)(2,1)S(1)} fusion(bf16[96,256,128]{2,1,0:T(8,128)(2,1)} %pad_maximum_fusion, s32[1024]{0:T(1024)S(1)} %get-tuple-element.52), kind=kCustom, calls=%fused_computation | custom fusion | bytes 262152 | tf_op jit(solution)/shard_map/gather | solution.py:52
  73.4 3.4 %gather_fusion.14 = bf16[2,256,128]{2,1,0:T(8,128)(2,1)S(1)} fusion(bf16[96,256,128]{2,1,0:T(8,128)(2,1)} %pad_maximum_fusion, s32[1024]{0:T(1024)S(1)} %get-tuple-element.45), kind=kCustom, calls=%fused_computation.14 | custom fusion | bytes 262152 | tf_op jit(solution)/shard_map/gather | solution.py:52
  77.0 0.1 fusion.56
  77.2 0.1 fusion.57
  77.3 0.1 fusion.58
  77.5 0.1 fusion.59
  77.6 0.1 fusion.60
  77.8 0.1 fusion.53
  77.9 0.2 convolution_multiply_fusion.10
  78.2 0.2 convolution_multiply_fusion.11
  78.4 0.2 convolution_multiply_fusion.12
  78.6 0.2 convolution_multiply_fusion.7
  78.9 0.2 convolution_multiply_fusion.8
  79.1 0.2 convolution_multiply_fusion.9
  79.4 0.2 convolution_multiply_fusion.6
  79.6 0.5 multiply_reduce_fusion
  80.1 0.7 fusion.6
  80.8 0.7 fusion.35
  81.5 0.6 fusion.21
  82.1 0.7 fusion.5
  82.8 0.7 fusion.71
  83.4 0.7 fusion.70
  84.1 0.7 fusion.4
  84.8 0.7 fusion.73
  85.4 0.7 fusion.72
  86.1 0.7 fusion.3
  86.8 0.7 fusion.75
  87.4 0.7 fusion.74
  88.1 0.7 fusion.2
  88.7 0.7 fusion.77
  89.4 0.7 fusion.76
  90.1 0.9 fusion.1
  91.0 0.7 convolution_divide_fusion
  91.7 0.5 fusion.51
  92.2 0.6 fusion.49
  92.8 0.7 fusion.16
  93.6 0.3 slice_bitcast_fusion
  95.5 18.3 %all_to_all.14 = bf16[16,16,2,128]{3,1,2,0:T(8,128)(2,1)S(1)} all-to-all(bf16[16,16,2,128]{3,1,2,0:T(8,128)(2,1)S(1)} %constant_dynamic-update-slice_fusion), channel_id=1, replica_groups=mesh['mem'=16,'lon'=16] {'mem'}, dimensions={0} | all-to-all | bytes 262144 | tf_op jit(solution)/shard_map/all_to_all | solution.py:81
  113.9 0.7 reshape_reshape.3
  (79 shorter events, 2.7 us)
Async XLA Ops:
  0.0 16.7 %copy-start = (bf16[16,4096]{1,0:T(8,128)(2,1)S(1)}, bf16[16,4096]{1,0:T(8,128)(2,1)}, u32[]{:S(2)}) copy-start(bf16[16,4096]{1,0:T(8,128)(2,1)} %param.6) | copy-start | bytes 393220
  0.0 26.7 %copy-start.2 = (s32[32,8]{0,1:T(8,128)S(1)}, s32[32,8]{0,1:T(8,128)}, u32[]{:S(2)}) copy-start(s32[32,8]{0,1:T(8,128)} %param.11) | copy-start | bytes 3076
  3.7 23.2 %collective-permute-start.2 = (bf16[32,2,128]{2,1,0:T(2,128)(2,1)S(1)}, bf16[32,2,128]{2,1,0:T(2,128)(2,1)S(1)}, u32[]{:S(2)}, u32[]{:S(2)}) collective-permute-start(bf16[32,2,128]{2,1,0:T(2,128)(2,1)S(1)} %pad_maximum_fusion.2), channel_id=1, source_target_pairs={{0,1},{1,2},{2,3},{3,4},{4,5},{5,6},{6,7},{7,8},{8,9},{9,10},{10,1... | collective-permute-start | bytes 49160 | tf_op jit(solution)/shard_map/ppermute | solution.py:18
  3.8 23.2 %collective-permute-start.3 = (bf16[32,2,128]{2,1,0:T(2,128)(2,1)S(1)}, bf16[32,2,128]{2,1,0:T(2,128)(2,1)S(1)}, u32[]{:S(2)}, u32[]{:S(2)}) collective-permute-start(bf16[32,2,128]{2,1,0:T(2,128)(2,1)S(1)} %pad_maximum_fusion.2), channel_id=1, source_target_pairs={{1,0},{2,1},{3,2},{4,3},{5,4},{6,5},{7,6},{8,7},{9,8},{10,9},{11,1... | collective-permute-start | bytes 49160 | tf_op jit(solution)/shard_map/ppermute | solution.py:19
  11.3 32.9 %collective-permute-start = (bf16[32,256,128]{2,1,0:T(8,128)(2,1)S(1)}, bf16[32,256,128]{2,1,0:T(8,128)(2,1)}, u32[]{:S(2)}, u32[]{:S(2)}) collective-permute-start(bf16[32,256,128]{2,1,0:T(8,128)(2,1)S(1)} %fusion), channel_id=1, source_target_pairs={{0,1},{1,2},{2,3},{3,4},{4,5},{5,6},{6,7},{7,8},{8,9},{9,10},{10,1... | collective-permute-start | bytes 6291464 | tf_op jit(solution)/shard_map/ppermute | solution.py:18
  11.4 32.8 %collective-permute-start.1 = (bf16[32,256,128]{2,1,0:T(8,128)(2,1)S(1)}, bf16[32,256,128]{2,1,0:T(8,128)(2,1)}, u32[]{:S(2)}, u32[]{:S(2)}) collective-permute-start(bf16[32,256,128]{2,1,0:T(8,128)(2,1)S(1)} %fusion), channel_id=1, source_target_pairs={{1,0},{2,1},{3,2},{4,3},{5,4},{6,5},{7,6},{8,7},{9,8},{10,9},{11,1... | collective-permute-start | bytes 6291464 | tf_op jit(solution)/shard_map/ppermute | solution.py:19
  17.4 25.9 %all-to-all-start = ((bf16[16,32,128]{2,0,1:T(8,128)(2,1)}), bf16[16,32,128]{2,0,1:T(8,128)(2,1)S(1)}, u32[]{:S(2)}, u32[]{:S(2)}) async-start(bf16[16,32,128]{2,0,1:T(8,128)(2,1)} %copy_bitcast_fusion), calls=%async_computation | async-start | bytes 262144 | tf_op jit(solution)/shard_map/all_to_all | solution.py:76
  86.8 6.1 %copy-start.1 = (f32[256,2,128]{2,0,1:T(8,128)S(1)}, f32[256,2,128]{2,0,1:T(8,128)}, u32[]{:S(2)}) copy-start(f32[256,2,128]{2,0,1:T(8,128)} %bitcast_subtract_fusion) | copy-start | bytes 786436
